TPU v7x, 32 devices: a whole 2x2x4 slice. The times are simulated.
32 devices in a mesh: seq: 8 (over z, x), head: 4 (over y, core).
Axes of the slice: x: 2, y: 2, z: 4, core: 2. Of those that a mesh axis runs over, the one named last changes fastest.
Arguments:
- queries: bfloat16 [3072, 1536], P('seq', 'head'), may hold values from -6 to 6
- key_vectors: bfloat16 [3072, 1536], P('seq', 'head'), may hold values from -6 to 6
- value_vectors: bfloat16 [3072, 1536], P('seq', 'head'), may hold values from -6 to 6
- out_weight: bfloat16 [1536, 5120], P('head'), may hold values from -0.15625 to 0.15625
- d_output: bfloat16 [3072, 5120], P('seq', 'head'), may hold values from -6 to 6
- block_keys: int32 [24, 24], replicated, may hold values from 0 to 23, as said below
- key_count: int32 [24], replicated, may hold values from 12 to 24
- frame_slot: int32 [8], replicated, may hold values from 0 to 7, each once
Outputs:
- layer_out: bfloat16 [3072, 5120], P('seq', 'head')
- d_query: bfloat16 [3072, 1536], P('seq', 'head')
- d_key: bfloat16 [3072, 1536], P('seq', 'head')
- d_value: bfloat16 [3072, 1536], P('seq', 'head')
- d_weight: bfloat16 [1536, 5120], P('head', 'seq')
Inputs may be any that keep to these rules, and one draw needn't show every extreme that they name: `block_keys`: row l names distinct logical key blocks for the logical query block l; the first 3 entries are the blocks of the query's own frame, the query block itself first; only the first key_count[l] entries are attended.
All inputs are finite; a program needn't handle non-finite values.
Results may differ from a plain program's by a relative error of at most 0.018.
Values may be sent and summed in bfloat16 or wider, within the bound.
A program may use at most 192 MiB of HBM per device.

v0:
```python
import math

import jax
import jax.numpy as jnp
from jax import lax
from jax.sharding import PartitionSpec as P

HD = 128
BLOCK = 128
FRAME_TOK = 384
NKB = 24


def storage_lists(block_keys, key_count, frame_slot):
    per_frame = FRAME_TOK // BLOCK
    frames = frame_slot.shape[0]
    block_count = block_keys.shape[0]
    frame_at = (
        jnp.zeros((frames,), jnp.int32).at[frame_slot].set(jnp.arange(frames, dtype=jnp.int32))
    )
    block_ids = jnp.arange(block_count, dtype=jnp.int32)
    logical = frame_at[block_ids // per_frame] * per_frame + block_ids % per_frame
    entries = block_keys[logical]
    counts = key_count[logical]
    stored = frame_slot[entries // per_frame] * per_frame + entries % per_frame
    return (stored, counts)


def head_columns(matrix, head_position):
    return matrix[:, head_position * HD : (head_position + 1) * HD]


def on_device(
    queries, key_vectors, value_vectors, out_weight, d_output, block_keys, key_count, frame_slot
):
    row_count, col_count = queries.shape
    head_count = col_count // HD
    block_count = block_keys.shape[0]
    local_blocks = row_count // BLOCK
    key_span = NKB * BLOCK
    score_scale = 1.0 / math.sqrt(HD)
    seq_index = lax.axis_index("seq")
    stored, counts = storage_lists(block_keys, key_count, frame_slot)
    first_block = seq_index * local_blocks
    my_lists = lax.dynamic_slice_in_dim(stored, first_block, local_blocks, 0)
    my_counts = lax.dynamic_slice_in_dim(counts, first_block, local_blocks, 0)
    flat_lists = my_lists.reshape(-1)
    whole_keys, whole_values = (
        lax.all_gather(key_vectors, "seq", axis=0, tiled=True),
        lax.all_gather(value_vectors, "seq", axis=0, tiled=True),
    )
    valid_keys = jnp.repeat(jnp.arange(NKB)[None, :] < my_counts[:, None], BLOCK, axis=1)
    query_for_head, head_keys, head_values, head_weights, head_attn, head_lse = (
        [],
        [],
        [],
        [],
        [],
        [],
    )
    for head_position in range(head_count):
        query_block_rows = head_columns(queries, head_position).reshape(local_blocks, BLOCK, HD)
        selected_keys = (
            head_columns(whole_keys, head_position)
            .reshape(block_count, BLOCK, HD)[my_lists]
            .reshape(local_blocks, key_span, HD)
        )
        selected_values = (
            head_columns(whole_values, head_position)
            .reshape(block_count, BLOCK, HD)[my_lists]
            .reshape(local_blocks, key_span, HD)
        )
        scores = (
            jnp.einsum(
                "xvz,xlz->xvl", query_block_rows, selected_keys, preferred_element_type=jnp.float32
            )
            * score_scale
        )
        scores = jnp.where(valid_keys[:, None, :], scores, -1e30)
        row_peak = jnp.max(scores, axis=-1, keepdims=True)
        exp_scores = jnp.exp(scores - row_peak)
        row_total = jnp.sum(exp_scores, axis=-1, keepdims=True)
        attn_weights = exp_scores / row_total
        reduced_precision_weights = attn_weights.astype(jnp.bfloat16)
        attn_blocks = jnp.einsum(
            "ycn,ynl->ycl",
            reduced_precision_weights,
            selected_values,
            preferred_element_type=jnp.float32,
        ).astype(jnp.bfloat16)
        query_for_head.append(query_block_rows)
        head_keys.append(selected_keys)
        head_values.append(selected_values)
        head_weights.append(attn_weights)
        head_attn.append(attn_blocks)
        head_lse.append((row_peak + jnp.log(row_total)).reshape(row_count))
    attn_flat = jnp.concatenate([piece.reshape(row_count, HD) for piece in head_attn], axis=1)
    layer_out = lax.psum_scatter(
        jnp.dot(attn_flat, out_weight, preferred_element_type=jnp.float32).astype(jnp.bfloat16),
        "head",
        scatter_dimension=1,
        tiled=True,
    )
    shard_cols = lax.all_gather(d_output, "head", axis=1, tiled=True)
    grad_accum = lax.dot_general(
        shard_cols, out_weight, (((1,), (1,)), ((), ())), preferred_element_type=jnp.float32
    )
    weight_part = lax.dot_general(
        attn_flat, shard_cols, (((0,), (0,)), ((), ())), preferred_element_type=jnp.float32
    )
    grad_accum, weight_term = (grad_accum, weight_part)
    d_attn = grad_accum.astype(jnp.bfloat16)
    d_weight = lax.psum_scatter(
        weight_term.astype(jnp.bfloat16), "seq", scatter_dimension=1, tiled=True
    )
    query_grads, key_parts, value_parts, head_delta = ([], [], [], [])
    for head_position in range(head_count):
        block_gradient_set = head_columns(d_attn, head_position).reshape(local_blocks, BLOCK, HD)
        attn_weights = head_weights[head_position]
        row_delta = jnp.sum(
            block_gradient_set.astype(jnp.float32) * head_attn[head_position].astype(jnp.float32),
            axis=-1,
        )
        grad_weights = jnp.einsum(
            "xvz,xlz->xvl",
            block_gradient_set,
            head_values[head_position],
            preferred_element_type=jnp.float32,
        )
        score_gradient = (attn_weights * (grad_weights - row_delta[..., None])).astype(jnp.bfloat16)
        grad_query = (
            jnp.einsum(
                "ycn,ynl->ycl",
                score_gradient,
                head_keys[head_position],
                preferred_element_type=jnp.float32,
            )
            * score_scale
        )
        query_grads.append(grad_query.astype(jnp.bfloat16).reshape(row_count, HD))
        head_delta.append(row_delta.reshape(row_count))
        reduced_precision_weights = attn_weights.astype(jnp.bfloat16)
        key_part = jnp.einsum(
            "nlj,nlh->njh",
            score_gradient,
            query_for_head[head_position],
            preferred_element_type=jnp.float32,
        ).reshape(local_blocks * NKB, BLOCK, HD)
        value_part = jnp.einsum(
            "nlj,nlh->njh",
            reduced_precision_weights,
            block_gradient_set,
            preferred_element_type=jnp.float32,
        ).reshape(local_blocks * NKB, BLOCK, HD)
        key_full = jnp.zeros((block_count, BLOCK, HD), jnp.float32).at[flat_lists].add(key_part)
        value_full = jnp.zeros((block_count, BLOCK, HD), jnp.float32).at[flat_lists].add(value_part)
        key_parts.append(key_full.reshape(block_count * BLOCK, HD))
        value_parts.append(value_full.reshape(block_count * BLOCK, HD))
    d_query = jnp.concatenate(query_grads, axis=1)
    key_sum, value_sum = (
        lax.psum_scatter(
            jnp.concatenate(key_parts, axis=1).astype(jnp.bfloat16),
            "seq",
            scatter_dimension=0,
            tiled=True,
        ).astype(jnp.float32),
        lax.psum_scatter(
            jnp.concatenate(value_parts, axis=1).astype(jnp.bfloat16),
            "seq",
            scatter_dimension=0,
            tiled=True,
        ).astype(jnp.float32),
    )
    d_key = (key_sum * score_scale).astype(jnp.bfloat16)
    d_value = value_sum.astype(jnp.bfloat16)
    return (layer_out, d_query, d_key, d_value, d_weight)


def solution(mesh):
    return jax.shard_map(
        on_device,
        mesh=mesh,
        in_specs=(
            P("seq", "head"),
            P("seq", "head"),
            P("seq", "head"),
            P("head", None),
            P("seq", "head"),
            P(),
            P(),
            P(),
        ),
        out_specs=(
            P("seq", "head"),
            P("seq", "head"),
            P("seq", "head"),
            P("seq", "head"),
            P("head", "seq"),
        ),
        check_vma=False,
    )
```

profile of v0, /device:TPU:9, one launch (start us, length us, event | category | flops | bytes accessed | tf_op | source)
XLA Modules:
  0.0 505.0 jit_solution(1043432755236806603)
XLA Ops:
  13.2 3.8 gather_fusion.3
  17.5 44.8 %all-gather.6.cloned.1.call-done = bf16[3072,384]{1,0:T(8,128)(2,1)} async-done(((bf16[384,384]{1,0:T(8,128)(2,1)}), bf16[3072,384]{1,0:T(8,128)(2,1)}) %all-gather.6.cloned.1.call-update) | async-done | bytes 2359312 | tf_op jit(solution)/shard_map/all_gather | solution.py:50
  66.5 48.6 %all-gather.4.cloned.1.call-done = bf16[3072,384]{1,0:T(8,128)(2,1)} async-done(((bf16[384,384]{1,0:T(8,128)(2,1)}), bf16[3072,384]{1,0:T(8,128)(2,1)}) %all-gather.4.cloned.1.call-update) | async-done | bytes 2359312 | tf_op jit(solution)/shard_map/all_gather | solution.py:49
  117.7 3.5 gather_fusion.8
  131.1 5.6 %fusion.48 = (f32[3,128]{1,0:T(4,128)S(1)}, f32[3,128,3072]{1,2,0:T(8,128)}) fusion(bf16[3,3072,128]{2,1,0:T(8,128)(2,1)} %bitcast.141, bf16[3,128,128]{2,1,0:T(8,128)(2,1)S(1)} %bitcast.175, pred[3,3072]{1,0:T(4,128)(4,1)S(1)} %bitcast.180), kind=kOutput, calls=%fused_computation.112 | convolution fusion | flops 306711552 | bytes 7186944 | tf_op jit(solution)/shard_map/sub | solution.py:81
  136.7 5.8 %fusion.47 = (f32[3,128]{1,0:T(4,128)S(1)}, f32[3,128,3072]{1,2,0:T(8,128)}) fusion(bf16[3,3072,128]{2,1,0:T(8,128)(2,1)} %bitcast.139, bf16[3,128,128]{2,1,0:T(8,128)(2,1)S(1)} %bitcast.173, pred[3,3072]{1,0:T(4,128)(4,1)S(1)} %bitcast.181), kind=kOutput, calls=%fused_computation.111 | convolution fusion | flops 306711552 | bytes 7186944 | tf_op jit(solution)/shard_map/sub | solution.py:81
  142.5 4.0 fusion.46
  155.3 5.7 %convolution_convert_fusion.2 = bf16[384,384]{1,0:T(8,128)(2,1)S(1)} fusion(bf16[384,5120]{1,0:T(8,128)(2,1)} %all-gather.8.cloned.1.call-done, bf16[384,5120]{1,0:T(8,128)(2,1)} %param.11), kind=kOutput, calls=%fused_computation.48 | convolution fusion | flops 1510096896 | bytes 8159232 | tf_op jit(solution)/shard_map/dot_general | solution.py:105
  162.0 3.2 multiply_convert_fusion.2
  165.2 3.0 fusion.49
  168.4 10.9 %scatter_fusion = f32[24,128,128]{2,1,0:T(8,128)S(1)} fusion(f32[24,128,128]{2,1,0:T(8,128)S(1)} %broadcast.238.clone.2, s32[72]{0:T(128)S(1)} %fusion.30, f32[72,128,128]{2,1,0:T(8,128)} %bitcast.127), kind=kCustom, calls=%fused_computation.11 | custom fusion | flops 1179648 | bytes 14156064 | tf_op jit(solution)/shard_map/scatter-add | solution.py:155
  183.7 3.2 multiply_convert_fusion.1
  190.1 10.7 %scatter_fusion.1 = f32[24,128,128]{2,1,0:T(8,128)S(1)} fusion(f32[24,128,128]{2,1,0:T(8,128)S(1)} %broadcast.238.clone.1, s32[72]{0:T(128)S(1)} %fusion.30, f32[72,128,128]{2,1,0:T(8,128)} %bitcast.128), kind=kCustom, calls=%fused_computation.12 | custom fusion | flops 1179648 | bytes 14156064 | tf_op jit(solution)/shard_map/scatter-add | solution.py:155
  205.2 3.2 multiply_convert_fusion
  211.5 10.7 %scatter_fusion.2 = f32[24,128,128]{2,1,0:T(8,128)S(1)} fusion(f32[24,128,128]{2,1,0:T(8,128)S(1)} %broadcast.238.clone, s32[72]{0:T(128)S(1)} %fusion.30, f32[72,128,128]{2,1,0:T(8,128)} %bitcast.129), kind=kCustom, calls=%fused_computation.13 | custom fusion | flops 1179648 | bytes 14156064 | tf_op jit(solution)/shard_map/scatter-add | solution.py:155
  224.1 6.2 %convolution_convert_fusion = bf16[384,5120]{1,0:T(8,128)(2,1)} fusion(bf16[384,5120]{1,0:T(8,128)(2,1)} %all-gather.8.cloned.1.call-done, bf16[384,128]{1,0:T(8,128)(2,1)S(1)} %bitcast.159, bf16[384,128]{1,0:T(8,128)(2,1)S(1)} %bitcast.157, bf16[384,128]{1,0:T(8,128)(2,1)S(1)} %bitcast.155), kind=kOutput, calls=%fused_computation.20 | convolution fusion | flops 1512800256 | bytes 8159232 | tf_op jit(solution)/shard_map/dot_general | solution.py:108
  230.3 6.3 %copy.49 = bf16[384,5120]{0,1:T(8,128)(2,1)} copy(bf16[384,5120]{1,0:T(8,128)(2,1)} %convolution_convert_fusion) | data formatting | bytes 7864320
  241.4 11.0 %scatter_fusion.3 = f32[24,128,128]{2,1,0:T(8,128)S(1)} fusion(f32[24,128,128]{2,1,0:T(8,128)S(1)} %broadcast.238.clone.5, s32[72]{0:T(128)S(1)} %fusion.30, f32[72,128,128]{2,1,0:T(8,128)} %bitcast.125), kind=kCustom, calls=%fused_computation.14 | custom fusion | flops 1179648 | bytes 14156064 | tf_op jit(solution)/shard_map/scatter-add | solution.py:156
  257.2 10.7 %scatter_fusion.4 = f32[24,128,128]{2,1,0:T(8,128)S(1)} fusion(f32[24,128,128]{2,1,0:T(8,128)S(1)} %broadcast.238.clone.4, s32[72]{0:T(128)S(1)} %fusion.30, f32[72,128,128]{2,1,0:T(8,128)} %bitcast.126), kind=kCustom, calls=%fused_computation.15 | custom fusion | flops 1179648 | bytes 14156064 | tf_op jit(solution)/shard_map/scatter-add | solution.py:156
  272.7 10.7 %scatter_fusion.5 = f32[24,128,128]{2,1,0:T(8,128)S(1)} fusion(f32[24,128,128]{2,1,0:T(8,128)S(1)} %broadcast.238.clone.3, s32[72]{0:T(128)S(1)} %fusion.30, f32[72,128,128]{2,1,0:T(8,128)} %bitcast.124), kind=kCustom, calls=%fused_computation.16 | custom fusion | flops 1179648 | bytes 14156064 | tf_op jit(solution)/shard_map/scatter-add | solution.py:156
  285.3 6.3 %convolution_convert_fusion.1 = bf16[384,5120]{1,0:T(8,128)(2,1)} fusion(bf16[384,5120]{1,0:T(8,128)(2,1)} %param.11, bf16[384,128]{1,0:T(8,128)(2,1)S(1)} %bitcast.160, bf16[384,128]{1,0:T(8,128)(2,1)S(1)} %bitcast.158, bf16[384,128]{1,0:T(8,128)(2,1)S(1)} %bitcast.156), kind=kOutput, calls=%fused_computation.21 | convolution fusion | flops 1512800256 | bytes 8159232 | tf_op jit(solution)/shard_map/dot_general | solution.py:99
  302.1 77.7 %reduce-scatter.13.cloned.1.call-done = bf16[640,384]{1,0:T(8,128)(2,1)} async-done(((bf16[5120,384]{1,0:T(8,128)(2,1)}), bf16[640,384]{1,0:T(8,128)(2,1)}) %reduce-scatter.13.cloned.1.call-update) | async-done | bytes 491536
  381.8 69.1 %reduce-scatter.11.cloned.1.call-done = bf16[384,384]{1,0:T(8,128)(2,1)} async-done(((bf16[3072,384]{1,0:T(8,128)(2,1)}), bf16[384,384]{1,0:T(8,128)(2,1)}) %reduce-scatter.11.cloned.1.call-update) | async-done | bytes 294928 | tf_op jit(solution)/shard_map/reduce_scatter | solution.py:167
  451.0 47.2 %reduce-scatter.7.cloned.1.call-done = bf16[384,1280]{1,0:T(8,128)(2,1)} async-done(((bf16[384,5120]{1,0:T(8,128)(2,1)}), bf16[384,1280]{1,0:T(8,128)(2,1)}) %reduce-scatter.7.cloned.1.call-update) | async-done | bytes 983056 | tf_op jit(solution)/shard_map/reduce_scatter | solution.py:98
  (152 shorter events, 78.3 us)
Async XLA Ops:
  7.2 4.3 copy-start
  7.2 6.0 %copy-start.2 = (s32[8]{0:T(128)S(1)}, s32[8]{0:T(128)}, u32[]{:S(2)}) copy-start(s32[8]{0:T(128)} %param.15) | copy-start | bytes 100
  7.2 5.0 copy-start.3
  7.2 55.1 %all-gather.6.cloned.1.call-start = ((), (), s32[]{:S(2)}) async-start(), calls=%async_computation.5 | async-start | bytes 2654208 | tf_op jit(solution)/shard_map/all_gather | solution.py:50
  7.9 107.2 %all-gather.4.cloned.1.call-start = ((), (), s32[]{:S(2)}) async-start(), calls=%async_computation.4 | async-start | bytes 2654208 | tf_op jit(solution)/shard_map/all_gather | solution.py:49
  8.7 146.6 %all-gather.8.cloned.1.call-start = ((), (), s32[]{:S(2)}) async-start(), calls=%async_computation.7 | async-start | bytes 4915200 | tf_op jit(solution)/shard_map/all_gather | solution.py:104
  9.4 290.9 %reduce-scatter.9.cloned.1.call-start = ((), (), s32[]{:S(2)}) async-start(), calls=%async_computation.8 | async-start | bytes 2654208 | tf_op jit(solution)/shard_map/reduce_scatter | solution.py:161
  13.2 4.1 copy-start.34
  17.4 113.7 %copy-start.32 = (bf16[384,128]{1,0:T(8,128)(2,1)}, bf16[384,128]{1,0:T(8,128)(2,1)S(1)}, u32[]{:S(2)}) copy-start(bf16[384,128]{1,0:T(8,128)(2,1)S(1)} %get-tuple-element.16) | copy-start | bytes 294916
  17.4 119.2 %copy-start.30 = (bf16[384,128]{1,0:T(8,128)(2,1)}, bf16[384,128]{1,0:T(8,128)(2,1)S(1)}, u32[]{:S(2)}) copy-start(bf16[384,128]{1,0:T(8,128)(2,1)S(1)} %get-tuple-element.18) | copy-start | bytes 294916
  17.4 125.0 %copy-start.28 = (bf16[384,128]{1,0:T(8,128)(2,1)}, bf16[384,128]{1,0:T(8,128)(2,1)S(1)}, u32[]{:S(2)}) copy-start(bf16[384,128]{1,0:T(8,128)(2,1)S(1)} %get-tuple-element.17) | copy-start | bytes 294916
  136.7 5.8 %copy-start.16 = (bf16[72,128,128]{2,1,0:T(8,128)(2,1)S(1)}, bf16[72,128,128]{2,1,0:T(8,128)(2,1)}, u32[]{:S(2)}) copy-start(bf16[72,128,128]{2,1,0:T(8,128)(2,1)} %gather_fusion.8) | copy-start | bytes 7077892
  146.4 3.8 copy-start.23
  149.3 11.7 %copy-start.8 = (bf16[3,128,3072]{1,2,0:T(8,128)(2,1)}, bf16[3,128,3072]{1,2,0:T(8,128)(2,1)S(1)}, u32[]{:S(2)}) copy-start(bf16[3,128,3072]{1,2,0:T(8,128)(2,1)S(1)} %fusion.18) | copy-start | bytes 7077892
  155.2 5.8 %copy-start.21 = (bf16[72,128,128]{2,1,0:T(8,128)(2,1)S(1)}, bf16[72,128,128]{2,1,0:T(8,128)(2,1)}, u32[]{:S(2)}) copy-start(bf16[72,128,128]{2,1,0:T(8,128)(2,1)} %gather_fusion.5) | copy-start | bytes 7077892
  161.0 22.7 %copy-start.24 = (bf16[384,128]{1,0:T(8,128)(2,1)}, bf16[384,128]{1,0:T(8,128)(2,1)S(1)}, u32[]{:S(2)}) copy-start(bf16[384,128]{1,0:T(8,128)(2,1)S(1)} %get-tuple-element.15) | copy-start | bytes 294916
  162.0 3.3 copy-start.33
  183.7 3.2 copy-start.31
  205.2 3.2 copy-start.29
  224.1 155.7 %reduce-scatter.13.cloned.1.call-start = ((), (), s32[]{:S(2)}) async-start(), calls=%async_computation.10 | async-start | bytes 4423680
  236.7 214.2 %reduce-scatter.11.cloned.1.call-start = ((), (), s32[]{:S(2)}) async-start(), calls=%async_computation.9 | async-start | bytes 2654208 | tf_op jit(solution)/shard_map/reduce_scatter | solution.py:167
  241.4 11.2 %copy-start.25 = (bf16[384,128]{1,0:T(8,128)(2,1)S(1)}, bf16[384,128]{1,0:T(8,128)(2,1)}, u32[]{:S(2)}) copy-start(bf16[384,128]{1,0:T(8,128)(2,1)} %copy-done.24) | copy-start | bytes 294916
  285.3 212.9 %reduce-scatter.7.cloned.1.call-start = ((), (), s32[]{:S(2)}) async-start(), calls=%async_computation.6 | async-start | bytes 4915200 | tf_op jit(solution)/shard_map/reduce_scatter | solution.py:98
  296.3 201.8 %copy-start.1 = (s32[24,24]{1,0:T(8,128)S(1)}, s32[24,24]{1,0:T(8,128)}, u32[]{:S(2)}) copy-start(s32[24,24]{1,0:T(8,128)} %param.13) | copy-start | bytes 6916
  (18 other events, 40.1 us)
Sparse Core Ops, SparseCore 0:
  10.2 52.0 all-gather.5
  64.5 50.6 all-gather.3
  116.7 33.0 all-gather.7
  224.2 66.7 reduce-scatter.8
  294.6 85.2 reduce-scatter.12
  384.1 66.7 reduce-scatter.10
  454.2 43.8 reduce-scatter.6
where the time goes:
time: 509 us; the launch traced here: 505 us
  waiting for transfers between devices  290 us (57%)
  other arithmetic  78.7 us (15%)
  matrix products  71.5 us (14%)
  local copies, waits for them, and re-layouts  50.1 us (10%)
  between operations  14.8 us (3%)
    unnamed x8, waiting for transfers between devices  79.9 us
    reduce_scatter x1, waiting for transfers between devices, on_device(): lax.psum_scatter(jnp.concatenate(value_parts, axis=1).astype(jnp.bfloat16...  69.1 us
    scatter-add x6, other arithmetic, on_device(): jnp.zeros((block_count, BLOCK, HD), jnp.float32).at[flat_lists]  64.7 us
    all_gather x1, waiting for transfers between devices, on_device(): lax.all_gather(key_vectors, 'seq', axis=0, tiled=True)  48.6 us
    reduce_scatter x1, waiting for transfers between devices, on_device(): lax.psum_scatter(jnp.dot(attn_flat, out_weight, preferred_element_type=jn...  47.2 us
    all_gather x1, waiting for transfers between devices, on_device(): lax.all_gather(value_vectors, 'seq', axis=0, tiled=True)  44.8 us
    unnamed x74, local copies, waits for them, and re-layouts  22.1 us
    sub x3, matrix products, on_device(): exp_scores = jnp.exp(scores - row_peak)  15.3 us
  transfers between devices with their start and end apart: 7, of which 5 were waited for; matrix products, arithmetic and copies ran while one was open for 24% of the time, Pallas kernels for 0%

commit v1 on v0

v1 whole, which is shorter than its diff:
```python
import functools
import math

import jax
import jax.numpy as jnp
from jax import lax
from jax.experimental import pallas as pl
from jax.experimental.pallas import tpu as pltpu
from jax.sharding import PartitionSpec as P

HD = 128
BLOCK = 128
FRAME_TOK = 384
PER_FRAME = FRAME_TOK // BLOCK
NZ = 4
NEG = -1e30
MESH = pl.DeviceIdType.MESH
VMEM = pl.BlockSpec(memory_space=pltpu.VMEM)
ANY = pl.BlockSpec(memory_space=pl.ANY)
f32 = jnp.float32
bf16 = jnp.bfloat16


def dot(a, b, ca, cb):
    return lax.dot_general(a, b, (((ca,), (cb,)), ((), ())), preferred_element_type=f32)


def line_barrier(nz, nx, z, x):
    barrier = pltpu.get_barrier_semaphore()
    for dz in range(1, nz):
        pl.semaphore_signal(
            barrier, inc=1, device_id={"seq": lax.rem(z + dz, nz) * nx + x}, device_id_type=MESH
        )
    for dx in range(1, nx):
        pl.semaphore_signal(
            barrier, inc=1, device_id={"seq": z * nx + lax.rem(x + dx, nx)}, device_id_type=MESH
        )
    pl.semaphore_wait(barrier, nz + nx - 2)


def gather_kernel(nz, nx, k_ref, v_ref, ko_ref, vo_ref, own_sem, zs, zr, xs, xr):
    me = lax.axis_index("seq")
    z, x = me // nx, lax.rem(me, nx)
    line_barrier(nz, nx, z, x)
    items = ((k_ref, ko_ref), (v_ref, vo_ref))
    started = []
    for i, (src, dst) in enumerate(items):
        for dx in range(1, nx):
            c = pltpu.make_async_remote_copy(
                src_ref=src, dst_ref=dst.at[me],
                send_sem=xs.at[i, 0, dx - 1], recv_sem=xr.at[i, 0, dx - 1],
                device_id={"seq": z * nx + lax.rem(x + dx, nx)}, device_id_type=MESH,
            )
            c.start()
            started.append(c)
        for dz in range(1, nz):
            c = pltpu.make_async_remote_copy(
                src_ref=src, dst_ref=dst.at[me],
                send_sem=zs.at[i, dz - 1], recv_sem=zr.at[i, dz - 1],
                device_id={"seq": lax.rem(z + dz, nz) * nx + x}, device_id_type=MESH,
            )
            c.start()
            started.append(c)
    own = []
    for i, (src, dst) in enumerate(items):
        c = pltpu.make_async_copy(src, dst.at[me], own_sem.at[i])
        c.start()
        own.append(c)
    for i, (src, dst) in enumerate(items):
        for dz in range(1, nz):
            s = lax.rem(z - dz + nz, nz) * nx + x
            pltpu.make_async_remote_copy(
                src_ref=src, dst_ref=dst.at[s],
                send_sem=zs.at[i, dz - 1], recv_sem=zr.at[i, dz - 1],
                device_id={"seq": s}, device_id_type=MESH,
            ).wait_recv()
            for dx in range(1, nx):
                c = pltpu.make_async_remote_copy(
                    src_ref=dst.at[s], dst_ref=dst.at[s],
                    send_sem=xs.at[i, dz, dx - 1], recv_sem=xr.at[i, dz, dx - 1],
                    device_id={"seq": z * nx + lax.rem(x + dx, nx)}, device_id_type=MESH,
                )
                c.start()
                started.append(c)
    for i, (src, dst) in enumerate(items):
        for dz in range(nz):
            for dx in range(1, nx):
                s = lax.rem(z - dz + nz, nz) * nx + lax.rem(x - dx + nx, nx)
                pltpu.make_async_remote_copy(
                    src_ref=src, dst_ref=dst.at[s],
                    send_sem=xs.at[i, dz, dx - 1], recv_sem=xr.at[i, dz, dx - 1],
                    device_id={"seq": z * nx + lax.rem(x + dx, nx)}, device_id_type=MESH,
                ).wait_recv()
    for c in started:
        c.wait_send()
    for c in own:
        c.wait()


def gather_rows(keys, values, n_seq):
    nz, nx = NZ, n_seq // NZ
    shape = jax.ShapeDtypeStruct((n_seq,) + keys.shape, keys.dtype)
    dma = pltpu.SemaphoreType.DMA
    return pl.pallas_call(
        functools.partial(gather_kernel, nz, nx),
        out_shape=(shape, shape),
        in_specs=[ANY, ANY],
        out_specs=(ANY, ANY),
        scratch_shapes=[
            dma((2,)), dma((2, nz - 1)), dma((2, nz - 1)), dma((2, nz, nx - 1)), dma((2, nz, nx - 1)),
        ],
        compiler_params=pltpu.CompilerParams(collective_id=0, has_side_effects=True),
    )(keys, values)


def scatter_kernel(nz, nx, scales, n, *refs):
    parts, outs = refs[:n], refs[n:2 * n]
    rx, sz, rz = refs[2 * n:3 * n], refs[3 * n:4 * n], refs[4 * n:5 * n]
    xs, xr, zs, zr = refs[5 * n:]
    me = lax.axis_index("seq")
    z, x = me // nx, lax.rem(me, nx)
    line_barrier(nz, nx, z, x)
    order = list(range(1, nz)) + [0]

    def piece(i, s):
        if len(parts[i].shape) == 3:
            return parts[i].at[s]
        width = outs[i].shape[1]
        return parts[i].at[:, pl.ds(pl.multiple_of(s * width, width), width)]

    def x_copy(i, dz, dx):
        px = lax.rem(x + dx, nx)
        return pltpu.make_async_remote_copy(
            src_ref=piece(i, lax.rem(z + dz, nz) * nx + px), dst_ref=rx[i].at[dz, dx - 1],
            send_sem=xs.at[i, dz, dx - 1], recv_sem=xr.at[i, dz, dx - 1],
            device_id={"seq": z * nx + px}, device_id_type=MESH,
        )

    def z_copy(i, dz):
        return pltpu.make_async_remote_copy(
            src_ref=sz[i].at[dz - 1], dst_ref=rz[i].at[dz - 1],
            send_sem=zs.at[i, dz - 1], recv_sem=zr.at[i, dz - 1],
            device_id={"seq": lax.rem(z + dz, nz) * nx + x}, device_id_type=MESH,
        )

    for i in range(n):
        for dz in order:
            for dx in range(1, nx):
                x_copy(i, dz, dx).start()
    for i in range(n):
        rows = outs[i].shape[0]
        for dz in order[:-1]:
            for dx in range(1, nx):
                x_copy(i, dz, dx).wait_recv()
            mine = piece(i, lax.rem(z + dz, nz) * nx + x)

            @pl.loop(0, rows // BLOCK)
            def _(r):
                at = pl.ds(pl.multiple_of(r * BLOCK, BLOCK), BLOCK)
                total = mine[at, :].astype(f32)
                for dx in range(1, nx):
                    total += rx[i][dz, dx - 1, at, :].astype(f32)
                sz[i][dz - 1, at, :] = total.astype(bf16)

            z_copy(i, dz).start()
    for i in range(n):
        rows = outs[i].shape[0]
        for dx in range(1, nx):
            x_copy(i, 0, dx).wait_recv()
        for dz in range(1, nz):
            z_copy(i, dz).wait_recv()
        mine = piece(i, me)

        @pl.loop(0, rows // BLOCK)
        def _(r):
            at = pl.ds(pl.multiple_of(r * BLOCK, BLOCK), BLOCK)
            total = mine[at, :].astype(f32)
            for dx in range(1, nx):
                total += rx[i][0, dx - 1, at, :].astype(f32)
            for dz in range(1, nz):
                total += rz[i][dz - 1, at, :].astype(f32)
            if scales[i] != 1.0:
                total = total * scales[i]
            outs[i][at, :] = total.astype(bf16)

    for i in range(n):
        for dz in range(nz):
            for dx in range(1, nx):
                x_copy(i, dz, dx).wait_send()
            if dz:
                z_copy(i, dz).wait_send()


def scatter_sum(parts, shapes, scales, n_seq, collective_id):
    nz, nx = NZ, n_seq // NZ
    n = len(parts)
    dma = pltpu.SemaphoreType.DMA
    return pl.pallas_call(
        functools.partial(scatter_kernel, nz, nx, scales, n),
        out_shape=tuple(jax.ShapeDtypeStruct(s, bf16) for s in shapes),
        in_specs=[VMEM] * n,
        out_specs=(VMEM,) * n,
        scratch_shapes=[pltpu.VMEM((nz, nx - 1) + s, bf16) for s in shapes]
        + [pltpu.VMEM((nz - 1,) + s, bf16) for s in shapes] * 2
        + [dma((n, nz, nx - 1)), dma((n, nz, nx - 1)), dma((n, nz - 1)), dma((n, nz - 1))],
        compiler_params=pltpu.CompilerParams(
            collective_id=collective_id, has_side_effects=True, vmem_limit_bytes=56 * 2**20
        ),
    )(*parts)


def attention_kernel(q_ref, k_ref, v_ref, g_ref, bias_ref, o_ref, dq_ref, dk_ref, dv_ref, e_ref):
    frames, rows, _ = k_ref.shape
    cols = q_ref.shape[0]
    scale = 1.0 / math.sqrt(HD)
    factor = scale * math.log2(math.e)
    q = q_ref[...]
    g = g_ref[...]

    def score_step(c, peak):
        s = dot(k_ref[c], q, 1, 1).reshape(PER_FRAME, BLOCK, cols) * factor
        s = (s + bias_ref[c][:, None, :]).reshape(rows, cols)
        e_ref[c] = s
        return jnp.maximum(peak, jnp.max(s.reshape(rows // 8, 8, cols), axis=0))

    peak = lax.fori_loop(0, frames, score_step, jnp.full((8, cols), NEG, f32))
    peak = jnp.max(peak, axis=0, keepdims=True)

    def sum_step(c, carry):
        total, out = carry
        e = jnp.exp2(e_ref[c] - peak)
        e_ref[c] = e
        total = total + jnp.sum(e.reshape(rows // 8, 8, cols), axis=0)
        out = out + dot(v_ref[c], e.astype(bf16), 0, 0)
        return total, out

    total, out = lax.fori_loop(
        0, frames, sum_step, (jnp.zeros((8, cols), f32), jnp.zeros((HD, cols), f32))
    )
    inverse = 1.0 / jnp.sum(total, axis=0, keepdims=True)
    out = (out * inverse).astype(bf16).astype(f32)
    o_ref[...] = out.T.astype(bf16)
    delta = jnp.sum(g.astype(f32).T * out, axis=0, keepdims=True)

    def grad_step(c, dq):
        w = e_ref[c] * inverse
        dv_ref[c] = dot(w.astype(bf16), g, 1, 0).astype(bf16)
        gw = dot(v_ref[c], g, 1, 1)
        ds = (w * (gw - delta)).astype(bf16)
        dk_ref[c] = dot(ds, q, 1, 0).astype(bf16)
        return dq + dot(k_ref[c], ds, 0, 0)

    dq = lax.fori_loop(0, frames, grad_step, jnp.zeros((HD, cols), f32))
    dq_ref[...] = (dq * scale).T.astype(bf16)


def attention(queries, keys, values, grads, bias):
    rows, width = queries.shape
    heads = width // HD
    by_head = pl.BlockSpec((rows, HD), lambda h: (0, h))
    whole = pl.BlockSpec((keys.shape[0], keys.shape[1], HD), lambda h: (0, 0, h))
    flops = 12 * rows * keys.shape[0] * keys.shape[1] * width
    return pl.pallas_call(
        attention_kernel,
        grid=(heads,),
        out_shape=(
            jax.ShapeDtypeStruct(queries.shape, bf16),
            jax.ShapeDtypeStruct(queries.shape, bf16),
            jax.ShapeDtypeStruct(keys.shape, bf16),
            jax.ShapeDtypeStruct(keys.shape, bf16),
        ),
        in_specs=[by_head, whole, whole, by_head, pl.BlockSpec(bias.shape, lambda h: (0, 0, 0))],
        out_specs=(by_head, by_head, whole, whole),
        scratch_shapes=[pltpu.VMEM((keys.shape[0], keys.shape[1], rows), f32)],
        compiler_params=pltpu.CompilerParams(vmem_limit_bytes=56 * 2**20),
        cost_estimate=pl.CostEstimate(
            flops=flops, bytes_accessed=4 * 2 * keys.size, transcendentals=flops // (12 * HD)
        ),
    )(queries, keys, values, grads, bias)


def mask_bias(block_keys, key_count, frame_slot, seq_index, local_blocks):
    frames = frame_slot.shape[0]
    block_count, entries_count = block_keys.shape
    ids = jnp.arange(frames, dtype=jnp.int32)
    local_frames = local_blocks // PER_FRAME
    slots = seq_index * local_frames + jnp.arange(local_frames, dtype=jnp.int32)
    frame_at = jnp.sum(jnp.where(frame_slot[None, :] == slots[:, None], ids[None, :], 0), axis=1)
    logical = (frame_at[:, None] * PER_FRAME + jnp.arange(PER_FRAME)[None, :]).reshape(-1)
    all_blocks = jnp.arange(block_count, dtype=jnp.int32)
    pick = logical[:, None] == all_blocks[None, :]
    entries = jnp.sum(jnp.where(pick[:, :, None], block_keys[None], 0), axis=1)
    counts = jnp.sum(jnp.where(pick, key_count[None, :], 0), axis=1)
    slot_of = jnp.sum(
        jnp.where((entries // PER_FRAME)[..., None] == ids, frame_slot, 0), axis=-1
    )
    stored = slot_of * PER_FRAME + entries % PER_FRAME
    attended = jnp.arange(entries_count)[None, :] < counts[:, None]
    hit = jnp.any((stored[..., None] == all_blocks) & attended[..., None], axis=1)
    bias = jnp.where(hit, 0.0, NEG).astype(f32).T
    return jnp.repeat(bias, BLOCK, axis=1).reshape(frames, PER_FRAME, local_blocks * BLOCK)


def on_device(n_seq, queries, keys, values, out_weight, d_output, block_keys, key_count, frame_slot):
    rows, width = queries.shape
    seq_index = lax.axis_index("seq")
    bias = mask_bias(block_keys, key_count, frame_slot, seq_index, rows // BLOCK)
    full_grad = lax.all_gather(d_output, "head", axis=1, tiled=True)
    all_keys, all_values = gather_rows(keys, values, n_seq)
    d_attn = dot(full_grad, out_weight, 1, 1).astype(bf16)
    attn, d_query, key_parts, value_parts = attention(queries, all_keys, all_values, d_attn, bias)
    layer_out = lax.psum_scatter(
        dot(attn, out_weight, 1, 0).astype(bf16), "head", scatter_dimension=1, tiled=True
    )
    weight_part = dot(attn, full_grad, 0, 0).astype(bf16)
    share = out_weight.shape[1] // n_seq
    if share % 128:
        weight_part = weight_part.reshape(width, n_seq, share).transpose(1, 0, 2)
    d_key, d_value, d_weight = scatter_sum(
        (key_parts, value_parts, weight_part),
        ((rows, width), (rows, width), (width, share)),
        (1.0 / math.sqrt(HD), 1.0, 1.0),
        n_seq,
        1,
    )
    return (layer_out, d_query, d_key, d_value, d_weight)


def solution(mesh):
    return jax.shard_map(
        functools.partial(on_device, mesh.shape["seq"]),
        mesh=mesh,
        in_specs=(
            P("seq", "head"),
            P("seq", "head"),
            P("seq", "head"),
            P("head", None),
            P("seq", "head"),
            P(),
            P(),
            P(),
        ),
        out_specs=(
            P("seq", "head"),
            P("seq", "head"),
            P("seq", "head"),
            P("seq", "head"),
            P("head", "seq"),
        ),
        check_vma=False,
    )
```

time: 509 us -> 258 us (0.51)
  waiting for transfers between devices: 290 us -> 0.74 us
  Pallas kernels: 0 us -> 211 us
  other arithmetic: 78.7 us -> 3.96 us
  matrix products: 71.5 us -> 17.6 us
  local copies, waits for them, and re-layouts: 50.1 us -> 7.03 us
    pallas_call x0 -> x3, Pallas kernels: none -> 211 us  [the longest x1 112 us: scatter_sum(): pl.pallas_call(functools.partial(scatter_kernel, nz, nx, scales, n), out_...]
    reduce_scatter x3 -> x1, waiting for transfers between devices: 116 us -> 0.02 us  [on_device(): lax.psum_scatter(dot(attn, out_weight, 1, 0).astype(bf16), 'head', scatte...]
    all_gather x3 -> x1, waiting for transfers between devices: 93.4 us -> 0.02 us  [on_device(): full_grad = lax.all_gather(d_output, 'head', axis=1, tiled=True)]
    unnamed x8 -> x2, waiting for transfers between devices: 79.9 us -> 0.7 us
    scatter-add x6 -> x0, other arithmetic: 64.7 us -> none  [on_device(): jnp.zeros((block_count, BLOCK, HD), jnp.float32).at[flat_lists]]
    dot_general x18 -> x3, matrix products: 56.2 us -> 17.6 us  [dot(): lax.dot_general(a, b, (((ca,), (cb,)), ((), ())), preferred_element_type=...]
    gather x10 -> x0, local copies, waits for them, and re-layouts: 21.5 us -> none  [the longest x3 8.44 us: on_device(): head_columns(whole_keys, head_position).reshape(block_count, BLOCK, HD)]
    unnamed x74 -> x7, local copies, waits for them, and re-layouts: 22.1 us -> 6.2 us
  transfers between devices with their start and end apart: 7 -> 2, of which waited for: 5 -> 0; matrix products, arithmetic and copies ran while one was open for 24% -> 4% of each run, Pallas kernels for 0% -> 71%
where the time goes in v1:
time: 258 us; the launch traced here: 255 us
  Pallas kernels  211 us (82%)
  matrix products  17.6 us (7%)
  between operations  14.8 us (6%)
  local copies, waits for them, and re-layouts  7.03 us (3%)
  other arithmetic  3.96 us (2%)
    pallas_call x1, Pallas kernels, scatter_sum(): pl.pallas_call(functools.partial(scatter_kernel, nz, nx, scales, n), out_...  112 us
    pallas_call x1, Pallas kernels, gather_rows(): pl.pallas_call(functools.partial(gather_kernel, nz, nx), out_shape=(shape...  69.7 us
    pallas_call x1, Pallas kernels, attention(): pl.pallas_call(attention_kernel, grid=(heads,), out_shape=(jax.ShapeDtype...  29.5 us
    dot_general x3, matrix products, dot(): lax.dot_general(a, b, (((ca,), (cb,)), ((), ())), preferred_element_type=...  17.6 us
    unnamed x7, local copies, waits for them, and re-layouts  6.2 us
  transfers between devices with their start and end apart: 2, of which 0 were waited for; matrix products, arithmetic and copies ran while one was open for 4% of the time, Pallas kernels for 71%

profile of v1, /device:TPU:9, one launch (start us, length us, event | category | flops | bytes accessed | tf_op | source)
XLA Modules:
  0.0 255.0 jit_solution(5797094562617539120)
XLA Ops:
  7.2 0.0 all-gather.2.cloned.1.call-start
  7.2 0.7 all-gather.2.cloned.1.call-update
  7.9 0.0 reduce-scatter.2.cloned.1.call-start
  7.9 1.3 fusion.4
  9.9 0.8 select_reduce_fusion.2
  10.7 0.1 iota_compare_fusion.3
  10.8 0.8 select_reduce_fusion
  11.6 0.7 select_reduce_fusion.1
  12.4 0.1 iota_compare_fusion.2
  12.5 0.1 fusion.1
  12.6 0.1 copy.13
  12.7 0.1 broadcast_in_dim.77
  12.8 0.7 reshape_reshape.3.bias_ref
  13.4 69.7 %shard_map.119 = (bf16[8,384,384]{2,1,0:T(8,128)(2,1)}, bf16[8,384,384]{2,1,0:T(8,128)(2,1)}) custom-call(bf16[384,384]{1,0:T(8,128)(2,1)} %k_ref.1, bf16[384,384]{1,0:T(8,128)(2,1)} %v_ref.1), custom_call_target="tpu_custom_call" | custom-call | tf_op jit(solution)/shard_map/pallas_call | solution.py:104
  83.1 6.2 %convolution_convert_fusion.2.g_ref = bf16[384,384]{1,0:T(8,128)(2,1)} fusion(bf16[384,5120]{1,0:T(8,128)(2,1)} %all-gather.2.cloned.1.call-done, bf16[384,5120]{1,0:T(8,128)(2,1)} %param.11), kind=kOutput, calls=%fused_computation.2 | convolution fusion | flops 1510096896 | bytes 8159232 | tf_op jit(solution)/shard_map/dot_general | solution.py:25
  89.4 29.5 %shard_map.120 = (bf16[384,384]{1,0:T(8,128)(2,1)}, bf16[384,384]{1,0:T(8,128)(2,1)}, bf16[8,384,384]{2,1,0:T(8,128)(2,1)}, bf16[8,384,384]{2,1,0:T(8,128)(2,1)}) custom-call(bf16[384,384]{1,0:T(8,128)(2,1)} %q_ref.1, bf16[8,384,384]{2,1,0:T(8,128)(2,1)} %get-tuple-element.14.k_ref, bf16[8,384,384]{2,1,0:T(8,128)(2,1)} %get-tuple-element.15.v_ref, ...), custom_call_target="tpu_custom_call" | custom-call | flops 5435817984 | bytes 9437184 | tf_op jit(solution)/shard_map/pallas_call | solution.py:263
  118.8 5.1 %convolution_convert_fusion.1 = bf16[384,5120]{1,0:T(8,128)(2,1)} fusion(bf16[384,384]{1,0:T(8,128)(2,1)} %get-tuple-element.16, bf16[384,5120]{1,0:T(8,128)(2,1)S(1)} %copy-done), kind=kOutput, calls=%fused_computation.1 | convolution fusion | flops 1511915520 | bytes 8159232 | tf_op jit(solution)/shard_map/dot_general | solution.py:25
  123.9 0.9 copy-done.1
  124.9 6.3 %convolution_convert_fusion.refs_2_ = bf16[384,5120]{1,0:T(8,128)(2,1)} fusion(bf16[384,384]{1,0:T(8,128)(2,1)S(1)} %copy-done.1, bf16[384,5120]{1,0:T(8,128)(2,1)} %all-gather.2.cloned.1.call-done), kind=kOutput, calls=%fused_computation | convolution fusion | flops 1511915520 | bytes 8159232 | tf_op jit(solution)/shard_map/dot_general | solution.py:25
  131.2 111.6 %shard_map.121 = (bf16[384,384]{1,0:T(8,128)(2,1)}, bf16[384,384]{1,0:T(8,128)(2,1)}, bf16[384,640]{1,0:T(8,128)(2,1)}) custom-call(bf16[8,384,384]{2,1,0:T(8,128)(2,1)} %get-tuple-element.18.refs_0_, bf16[8,384,384]{2,1,0:T(8,128)(2,1)} %get-tuple-element.19.refs_1_, bf16[384,5120]{1,0:T(8,128)(2,1)} %convolution_convert_fusion.refs_2_), custom_call_target="tpu_custom_call" | custom-call | tf_op jit(solution)/shard_map/pallas_call | solution.py:198
  242.8 0.0 reduce-scatter.2.cloned.1.call-done
  242.9 1.7 copy.17
  244.6 1.7 copy.18
  246.3 1.8 copy.19
  (9 shorter events, 0.1 us)
Async XLA Ops:
  7.2 76.0 %all-gather.2.cloned.1.call-start = ((), (), s32[]{:S(2)}) async-start(), calls=%async_computation.1 | async-start | bytes 4915200 | tf_op jit(solution)/shard_map/all_gather | solution.py:308
  7.9 234.9 %reduce-scatter.2.cloned.1.call-start = ((), (), s32[]{:S(2)}) async-start(), calls=%async_computation.2 | async-start | bytes 4915200 | tf_op jit(solution)/shard_map/reduce_scatter | solution.py:312
  89.4 29.5 %copy-start = (bf16[384,5120]{1,0:T(8,128)(2,1)S(1)}, bf16[384,5120]{1,0:T(8,128)(2,1)}, u32[]{:S(2)}) copy-start(bf16[384,5120]{1,0:T(8,128)(2,1)} %param.11) | copy-start | bytes 11796484
  123.9 1.0 copy-start.1
Sparse Core Ops, SparseCore 0:
  9.6 34.5 all-gather.1
  124.0 42.2 reduce-scatter.1

commit v2 on v1

v2 whole, which is shorter than its diff:
```python
import functools
import math

import jax
import jax.numpy as jnp
from jax import lax
from jax.experimental import pallas as pl
from jax.experimental.pallas import tpu as pltpu
from jax.sharding import PartitionSpec as P

HD = 128
BLOCK = 128
FRAME_TOK = 384
PER_FRAME = FRAME_TOK // BLOCK
NZ = 4
NEG = -1e30
MESH = pl.DeviceIdType.MESH
VMEM = pl.BlockSpec(memory_space=pltpu.VMEM)
ANY = pl.BlockSpec(memory_space=pl.ANY)
f32 = jnp.float32
bf16 = jnp.bfloat16


def dot(a, b, ca, cb):
    return lax.dot_general(a, b, (((ca,), (cb,)), ((), ())), preferred_element_type=f32)


def line_barrier(nz, nx, z, x):
    barrier = pltpu.get_barrier_semaphore()
    for dz in range(1, nz):
        pl.semaphore_signal(
            barrier, inc=1, device_id={"seq": lax.rem(z + dz, nz) * nx + x}, device_id_type=MESH
        )
    for dx in range(1, nx):
        pl.semaphore_signal(
            barrier, inc=1, device_id={"seq": z * nx + lax.rem(x + dx, nx)}, device_id_type=MESH
        )
    pl.semaphore_wait(barrier, nz + nx - 2)


def gather_kernel(nz, nx, k_ref, v_ref, ko_ref, vo_ref, own_sem, zs, zr, xs, xr):
    me = lax.axis_index("seq")
    z, x = me // nx, lax.rem(me, nx)
    line_barrier(nz, nx, z, x)
    items = ((k_ref, ko_ref), (v_ref, vo_ref))
    started = []
    for i, (src, dst) in enumerate(items):
        for dx in range(1, nx):
            c = pltpu.make_async_remote_copy(
                src_ref=src, dst_ref=dst.at[me],
                send_sem=xs.at[i, 0, dx - 1], recv_sem=xr.at[i, 0, dx - 1],
                device_id={"seq": z * nx + lax.rem(x + dx, nx)}, device_id_type=MESH,
            )
            c.start()
            started.append(c)
        for dz in range(1, nz):
            c = pltpu.make_async_remote_copy(
                src_ref=src, dst_ref=dst.at[me],
                send_sem=zs.at[i, dz - 1], recv_sem=zr.at[i, dz - 1],
                device_id={"seq": lax.rem(z + dz, nz) * nx + x}, device_id_type=MESH,
            )
            c.start()
            started.append(c)
    own = []
    for i, (src, dst) in enumerate(items):
        c = pltpu.make_async_copy(src, dst.at[me], own_sem.at[i])
        c.start()
        own.append(c)
    for i, (src, dst) in enumerate(items):
        for dz in range(1, nz):
            s = lax.rem(z - dz + nz, nz) * nx + x
            pltpu.make_async_remote_copy(
                src_ref=src, dst_ref=dst.at[s],
                send_sem=zs.at[i, dz - 1], recv_sem=zr.at[i, dz - 1],
                device_id={"seq": s}, device_id_type=MESH,
            ).wait_recv()
            for dx in range(1, nx):
                c = pltpu.make_async_remote_copy(
                    src_ref=dst.at[s], dst_ref=dst.at[s],
                    send_sem=xs.at[i, dz, dx - 1], recv_sem=xr.at[i, dz, dx - 1],
                    device_id={"seq": z * nx + lax.rem(x + dx, nx)}, device_id_type=MESH,
                )
                c.start()
                started.append(c)
    for i, (src, dst) in enumerate(items):
        for dz in range(nz):
            for dx in range(1, nx):
                s = lax.rem(z - dz + nz, nz) * nx + lax.rem(x - dx + nx, nx)
                pltpu.make_async_remote_copy(
                    src_ref=src, dst_ref=dst.at[s],
                    send_sem=xs.at[i, dz, dx - 1], recv_sem=xr.at[i, dz, dx - 1],
                    device_id={"seq": z * nx + lax.rem(x + dx, nx)}, device_id_type=MESH,
                ).wait_recv()
    for c in started:
        c.wait_send()
    for c in own:
        c.wait()


def gather_rows(keys, values, n_seq):
    nz, nx = NZ, n_seq // NZ
    shape = jax.ShapeDtypeStruct((n_seq,) + keys.shape, keys.dtype)
    dma = pltpu.SemaphoreType.DMA
    return pl.pallas_call(
        functools.partial(gather_kernel, nz, nx),
        out_shape=(shape, shape),
        in_specs=[ANY, ANY],
        out_specs=(ANY, ANY),
        scratch_shapes=[
            dma((2,)), dma((2, nz - 1)), dma((2, nz - 1)), dma((2, nz, nx - 1)), dma((2, nz, nx - 1)),
        ],
        compiler_params=pltpu.CompilerParams(collective_id=0, has_side_effects=True),
    )(keys, values)


def head(h):
    return slice(h * HD, (h + 1) * HD)


def forward_kernel(q_ref, k_ref, v_ref, bias_ref, o_ref, ot_ref, lse_ref, e_ref):
    frames, rows, _ = k_ref.shape
    cols = q_ref.shape[0]
    q = q_ref[...]

    def score_step(c, peak):
        s = scores(k_ref[c], q, bias_ref[c])
        e_ref[c] = s
        return jnp.maximum(peak, jnp.max(s.reshape(rows // 8, 8, cols), axis=0))

    peak = lax.fori_loop(0, frames, score_step, jnp.full((8, cols), NEG, f32))
    peak = jnp.max(peak, axis=0, keepdims=True)

    def sum_step(c, carry):
        total, out = carry
        e = jnp.exp2(e_ref[c] - peak)
        total = total + jnp.sum(e.reshape(rows // 8, 8, cols), axis=0)
        out = out + dot(v_ref[c], e.astype(bf16), 0, 0)
        return total, out

    total, out = lax.fori_loop(
        0, frames, sum_step, (jnp.zeros((8, cols), f32), jnp.zeros((HD, cols), f32))
    )
    total = jnp.sum(total, axis=0, keepdims=True)
    out = out / total
    ot_ref[...] = out.astype(bf16)
    o_ref[...] = out.T.astype(bf16)
    lse_ref[0] = jnp.broadcast_to(peak + jnp.log2(total), (8, cols))


def scores(k, q, bias):
    rows, cols = k.shape[0], q.shape[0]
    factor = math.log2(math.e) / math.sqrt(HD)
    s = dot(k, q, 1, 1).reshape(PER_FRAME, BLOCK, cols) * factor
    return (s + bias[:, None, :]).reshape(rows, cols)


def forward(queries, keys, values, bias):
    rows, width = queries.shape
    heads = width // HD
    by_head = pl.BlockSpec((rows, HD), lambda h: (0, h))
    whole = pl.BlockSpec((keys.shape[0], keys.shape[1], HD), lambda h: (0, 0, h))
    flops = 4 * rows * keys.size
    return pl.pallas_call(
        forward_kernel,
        grid=(heads,),
        out_shape=(
            jax.ShapeDtypeStruct(queries.shape, bf16),
            jax.ShapeDtypeStruct((width, rows), bf16),
            jax.ShapeDtypeStruct((heads, 8, rows), f32),
        ),
        in_specs=[by_head, whole, whole, pl.BlockSpec(bias.shape, lambda h: (0, 0, 0))],
        out_specs=(
            by_head,
            pl.BlockSpec((HD, rows), lambda h: (h, 0)),
            pl.BlockSpec((1, 8, rows), lambda h: (h, 0, 0)),
        ),
        scratch_shapes=[pltpu.VMEM((keys.shape[0], keys.shape[1], rows), f32)],
        compiler_params=pltpu.CompilerParams(vmem_limit_bytes=48 * 2**20),
        cost_estimate=pl.CostEstimate(
            flops=flops, bytes_accessed=4 * keys.size, transcendentals=flops // (4 * HD)
        ),
    )(queries, keys, values, bias)


def backward_kernel(
    nz, nx, nh,
    q_ref, k_ref, v_ref, o_ref, ot_ref, lse_ref, bias_ref, grad_ref, ow_ref,
    layer_ref, dq_ref, dk_ref, dv_ref, dw_ref,
    wp, kp, vp, wx, kx, vx, wz, kz, vz, lp, lr, g_ref, acc, stat,
    xs, xr, zs, zr, ls, lrs,
):
    me = lax.axis_index("seq")
    hd = lax.axis_index("head")
    z, x = me // nx, lax.rem(me, nx)
    n_seq = nz * nx
    rows, width = q_ref.shape
    heads = width // HD
    scale = 1.0 / math.sqrt(HD)
    parts, rx, rz, outs = (wp, kp, vp), (wx, kx, vx), (wz, kz, vz), (dw_ref, dk_ref, dv_ref)

    barrier = pltpu.get_barrier_semaphore()
    for dz in range(1, nz):
        pl.semaphore_signal(
            barrier, inc=1, device_id={"seq": lax.rem(z + dz, nz) * nx + x}, device_id_type=MESH
        )
    for dx in range(1, nx):
        pl.semaphore_signal(
            barrier, inc=1, device_id={"seq": z * nx + lax.rem(x + dx, nx)}, device_id_type=MESH
        )
    for dh in range(1, nh):
        pl.semaphore_signal(
            barrier, inc=1, device_id={"head": lax.rem(hd + dh, nh)}, device_id_type=MESH
        )
    pl.semaphore_wait(barrier, nz + nx + nh - 3)

    def x_copy(i, dz, dx):
        px = lax.rem(x + dx, nx)
        return pltpu.make_async_remote_copy(
            src_ref=parts[i].at[lax.rem(z + dz, nz) * nx + px], dst_ref=rx[i].at[dz, dx - 1],
            send_sem=xs.at[i, dz, dx - 1], recv_sem=xr.at[i, dz, dx - 1],
            device_id={"seq": z * nx + px}, device_id_type=MESH,
        )

    def z_copy(i, dz):
        to = lax.rem(z + dz, nz) * nx + x
        return pltpu.make_async_remote_copy(
            src_ref=parts[i].at[to], dst_ref=rz[i].at[dz - 1],
            send_sem=zs.at[i, dz - 1], recv_sem=zr.at[i, dz - 1],
            device_id={"seq": to}, device_id_type=MESH,
        )

    def l_copy(dh):
        return pltpu.make_async_remote_copy(
            src_ref=lp.at[dh], dst_ref=lr.at[dh - 1],
            send_sem=ls.at[dh - 1], recv_sem=lrs.at[dh - 1],
            device_id={"head": lax.rem(hd + dh, nh)}, device_id_type=MESH,
        )

    def step(u):
        dz = lax.rem(u // nx + 1, nz)
        dx = lax.rem(lax.rem(u, nx) + 1, nx)
        return dz, dx, lax.rem(z + dz, nz) * nx + lax.rem(x + dx, nx)

    def forward_sum(i, dz):
        for dx in range(1, nx):
            x_copy(i, dz, dx).wait_recv()
        s = lax.rem(z + dz, nz) * nx + x

        @pl.loop(0, outs[i].shape[0] // BLOCK)
        def _(r):
            at = pl.ds(pl.multiple_of(r * BLOCK, BLOCK), BLOCK)
            total = parts[i][s, at, :].astype(f32)
            for dx in range(1, nx):
                total += rx[i][dz, dx - 1, at, :].astype(f32)
            parts[i][s, at, :] = total.astype(bf16)

        z_copy(i, dz).start()

    def last_sum(i, factor):
        for dx in range(1, nx):
            x_copy(i, 0, dx).wait_recv()
        for dz in range(1, nz):
            z_copy(i, dz).wait_recv()

        @pl.loop(0, outs[i].shape[0] // BLOCK)
        def _(r):
            at = pl.ds(pl.multiple_of(r * BLOCK, BLOCK), BLOCK)
            total = parts[i][me, at, :].astype(f32)
            for dx in range(1, nx):
                total += rx[i][0, dx - 1, at, :].astype(f32)
            for dz in range(1, nz):
                total += rz[i][dz - 1, at, :].astype(f32)
            outs[i][at, :] = (total * factor).astype(bf16)

    share = dw_ref.shape[1]
    group = math.lcm(share, 128) // share

    def weight_part(p):
        span = group * share
        r = jnp.dot(
            ot_ref[...],
            grad_ref[:, pl.ds(pl.multiple_of(p * span, 128), span)],
            preferred_element_type=f32,
        ).astype(bf16)
        for t in range(group):
            wp[p * group + t] = r[:, t * share:(t + 1) * share]

    if group > 1:
        pl.loop(0, n_seq // group)(weight_part)

    @pl.loop(0, n_seq)
    def _(u):
        dz, dx, s = step(u)
        if group == 1:
            weight_part(s)

        @pl.when(dx > 0)
        def _():
            x_copy(0, dz, dx).start()

    lw = layer_ref.shape[1]

    @pl.loop(0, nh)
    def _(j):
        dh = lax.rem(j + 1, nh)
        at = pl.ds(pl.multiple_of(lax.rem(hd + dh, nh) * lw, 128), lw)
        lp[dh] = jnp.dot(o_ref[...], ow_ref[:, at], preferred_element_type=f32).astype(bf16)

        @pl.when(dh > 0)
        def _():
            l_copy(dh).start()

    acc[...] = jnp.zeros_like(acc)
    chunk = 640

    @pl.loop(0, grad_ref.shape[1] // chunk)
    def _(c):
        at = pl.ds(pl.multiple_of(c * chunk, 128), chunk)
        acc[...] += dot(grad_ref[:, at], ow_ref[:, at], 1, 1)

    g_ref[...] = acc[...].astype(bf16)
    acc[...] = jnp.zeros_like(acc)
    for h in range(heads):
        gt = g_ref[:, head(h)].astype(f32).T
        stat[h] = jnp.broadcast_to(
            jnp.sum(gt * ot_ref[head(h), :].astype(f32), axis=0, keepdims=True), (8, rows)
        )

    @pl.loop(0, n_seq)
    def _(u):
        dz, dx, s = step(u)
        for h in range(heads):
            q, g = q_ref[:, head(h)], g_ref[:, head(h)]
            k, v = k_ref[s, :, head(h)], v_ref[s, :, head(h)]
            w = jnp.exp2(scores(k, q, bias_ref[s]) - lse_ref[h, 0:1, :])
            vp[s, :, head(h)] = dot(w.astype(bf16), g, 1, 0).astype(bf16)
            ds = (w * (dot(v, g, 1, 1) - stat[h, 0:1, :])).astype(bf16)
            kp[s, :, head(h)] = dot(ds, q, 1, 0).astype(bf16)
            acc[head(h), :] += dot(k, ds, 0, 0)

        @pl.when(dx > 0)
        def _():
            x_copy(1, dz, dx).start()
            x_copy(2, dz, dx).start()

        @pl.when((dx == 0) & (dz > 0))
        def _():
            forward_sum(0, dz)

    dq_ref[...] = (acc[...] * scale).T.astype(bf16)

    @pl.loop(1, nz)
    def _(dz):
        forward_sum(1, dz)
        forward_sum(2, dz)

    @pl.loop(1, nh)
    def _(dh):
        l_copy(dh).wait_recv()

    @pl.loop(0, rows // BLOCK)
    def _(r):
        at = pl.ds(pl.multiple_of(r * BLOCK, BLOCK), BLOCK)
        total = lp[0, at, :].astype(f32)
        for dh in range(1, nh):
            total += lr[dh - 1, at, :].astype(f32)
        layer_ref[at, :] = total.astype(bf16)

    last_sum(0, 1.0)
    last_sum(1, scale)
    last_sum(2, 1.0)
    for i in range(3):
        for dz in range(nz):
            for dx in range(1, nx):
                x_copy(i, dz, dx).wait_send()
            if dz:
                z_copy(i, dz).wait_send()
    for dh in range(1, nh):
        l_copy(dh).wait_send()


def backward(n_seq, nh, queries, keys, values, attn, attn_t, lse, bias, full_grad, out_weight):
    nz, nx = NZ, n_seq // NZ
    rows, width = queries.shape
    columns = out_weight.shape[1]
    shapes = ((width, columns // n_seq), (rows, width), (rows, width))
    dma = pltpu.SemaphoreType.DMA
    x_sem, z_sem, l_sem = dma((3, nz, nx - 1)), dma((3, nz - 1)), dma((nh - 1,))
    one = jax.ShapeDtypeStruct((rows, width), bf16)
    return pl.pallas_call(
        functools.partial(backward_kernel, nz, nx, nh),
        out_shape=(
            jax.ShapeDtypeStruct((rows, columns // nh), bf16),
            one,
            one,
            one,
            jax.ShapeDtypeStruct(shapes[0], bf16),
        ),
        in_specs=[VMEM] * 9,
        out_specs=(VMEM,) * 5,
        scratch_shapes=[pltpu.VMEM((n_seq,) + s, bf16) for s in shapes]
        + [pltpu.VMEM((nz, nx - 1) + s, bf16) for s in shapes]
        + [pltpu.VMEM((nz - 1,) + s, bf16) for s in shapes]
        + [
            pltpu.VMEM((nh, rows, columns // nh), bf16),
            pltpu.VMEM((nh - 1, rows, columns // nh), bf16),
            pltpu.VMEM((rows, width), bf16),
            pltpu.VMEM((width, rows), f32),
            pltpu.VMEM((width // HD, 8, rows), f32),
        ]
        + [x_sem, x_sem, z_sem, z_sem, l_sem, l_sem],
        compiler_params=pltpu.CompilerParams(
            collective_id=1, has_side_effects=True, vmem_limit_bytes=60 * 2**20
        ),
    )(queries, keys, values, attn, attn_t, lse, bias, full_grad, out_weight)


def mask_bias(block_keys, key_count, frame_slot, seq_index, local_blocks):
    frames = frame_slot.shape[0]
    block_count, entries_count = block_keys.shape
    ids = jnp.arange(frames, dtype=jnp.int32)
    local_frames = local_blocks // PER_FRAME
    slots = seq_index * local_frames + jnp.arange(local_frames, dtype=jnp.int32)
    frame_at = jnp.sum(jnp.where(frame_slot[None, :] == slots[:, None], ids[None, :], 0), axis=1)
    logical = (frame_at[:, None] * PER_FRAME + jnp.arange(PER_FRAME)[None, :]).reshape(-1)
    all_blocks = jnp.arange(block_count, dtype=jnp.int32)
    pick = logical[:, None] == all_blocks[None, :]
    entries = jnp.sum(jnp.where(pick[:, :, None], block_keys[None], 0), axis=1)
    counts = jnp.sum(jnp.where(pick, key_count[None, :], 0), axis=1)
    slot_of = jnp.sum(
        jnp.where((entries // PER_FRAME)[..., None] == ids, frame_slot, 0), axis=-1
    )
    stored = slot_of * PER_FRAME + entries % PER_FRAME
    attended = jnp.arange(entries_count)[None, :] < counts[:, None]
    hit = jnp.any((stored[..., None] == all_blocks) & attended[..., None], axis=1)
    bias = jnp.where(hit, 0.0, NEG).astype(f32).T
    return jnp.repeat(bias, BLOCK, axis=1).reshape(frames, PER_FRAME, local_blocks * BLOCK)


def on_device(
    n_seq, n_head,
    queries, keys, values, out_weight, d_output, block_keys, key_count, frame_slot,
):
    rows, width = queries.shape
    seq_index = lax.axis_index("seq")
    bias = mask_bias(block_keys, key_count, frame_slot, seq_index, rows // BLOCK)
    full_grad = lax.all_gather(d_output, "head", axis=1, tiled=True)
    all_keys, all_values = gather_rows(keys, values, n_seq)
    attn, attn_t, lse = forward(queries, all_keys, all_values, bias)
    return backward(
        n_seq, n_head, queries, all_keys, all_values, attn, attn_t, lse, bias, full_grad, out_weight
    )


def solution(mesh):
    return jax.shard_map(
        functools.partial(on_device, mesh.shape["seq"], mesh.shape["head"]),
        mesh=mesh,
        in_specs=(
            P("seq", "head"),
            P("seq", "head"),
            P("seq", "head"),
            P("head", None),
            P("seq", "head"),
            P(),
            P(),
            P(),
        ),
        out_specs=(
            P("seq", "head"),
            P("seq", "head"),
            P("seq", "head"),
            P("seq", "head"),
            P("head", "seq"),
        ),
        check_vma=False,
    )
```

time: 258 us -> 237 us (0.919)
  matrix products: 17.6 us -> 0 us
  Pallas kernels: 211 us -> 202 us
  local copies, waits for them, and re-layouts: 7.03 us -> 14.7 us
    dot_general x3 -> x0, matrix products: 17.6 us -> none  [dot(): lax.dot_general(a, b, (((ca,), (cb,)), ((), ())), preferred_element_type=...]
    pallas_call x2, Pallas kernels: 141 us -> 132 us  [the longest x1 118 us: backward(): pl.pallas_call(functools.partial(backward_kernel, nz, nx, nh), out_shape=...]
    unnamed x7 -> x21, local copies, waits for them, and re-layouts: 6.2 us -> 14.5 us
  transfers between devices with their start and end apart: 2 -> 1, of which waited for: 0 -> 0; matrix products, arithmetic and copies ran while one was open for 4% -> 2% of each run, Pallas kernels for 71% -> 36%
where the time goes in v2:
time: 237 us; the launch traced here: 236 us
  Pallas kernels  202 us (85%)
  between operations  14.8 us (6%)
  local copies, waits for them, and re-layouts  14.7 us (6%)
  other arithmetic  3.96 us (2%)
    pallas_call x1, Pallas kernels, backward(): pl.pallas_call(functools.partial(backward_kernel, nz, nx, nh), out_shape=...  118 us
    pallas_call x1, Pallas kernels, gather_rows(): pl.pallas_call(functools.partial(gather_kernel, nz, nx), out_shape=(shape...  69.7 us
    unnamed x21, local copies, waits for them, and re-layouts  14.5 us
    pallas_call x1, Pallas kernels, forward(): pl.pallas_call(forward_kernel, grid=(heads,), out_shape=(jax.ShapeDtypeSt...  14.3 us
  transfers between devices with their start and end apart: 1, of which 0 were waited for; matrix products, arithmetic and copies ran while one was open for 2% of the time, Pallas kernels for 36%

profile of v2, /device:TPU:9, one launch (start us, length us, event | category | flops | bytes accessed | tf_op | source)
XLA Modules:
  0.0 236.1 jit_solution(18396160245087704893)
XLA Ops:
  7.2 0.7 all-gather.2.cloned.1.call-update
  7.9 1.3 fusion.4
  9.9 0.8 select_reduce_fusion.2
  10.7 0.1 iota_compare_fusion.3
  10.8 0.8 select_reduce_fusion
  11.6 0.7 select_reduce_fusion.1
  12.3 0.1 iota_compare_fusion.2
  12.4 0.1 fusion.1
  12.5 0.1 copy.13
  12.6 0.1 broadcast_in_dim.77
  12.8 69.7 %shard_map.119 = (bf16[8,384,384]{2,1,0:T(8,128)(2,1)}, bf16[8,384,384]{2,1,0:T(8,128)(2,1)}) custom-call(bf16[384,384]{1,0:T(8,128)(2,1)} %k_ref.1, bf16[384,384]{1,0:T(8,128)(2,1)} %v_ref.1), custom_call_target="tpu_custom_call" | custom-call | tf_op jit(solution)/shard_map/pallas_call | solution.py:104
  82.5 1.7 copy-done
  84.2 1.7 copy-done.1
  85.9 1.0 copy-done.2
  86.8 14.3 %shard_map.120 = (bf16[384,384]{1,0:T(8,128)(2,1)S(1)}, bf16[384,384]{1,0:T(8,128)(2,1)S(1)}, f32[3,8,384]{2,1,0:T(8,128)S(1)}) custom-call(bf16[384,384]{1,0:T(8,128)(2,1)S(1)} %copy-done.2, bf16[8,384,384]{2,1,0:T(8,128)(2,1)S(1)} %copy-done, bf16[8,384,384]{2,1,0:T(8,128)(2,1)S(1)} %copy-done.1, f32[8,3,384]{2,1,0:T(4,128)S(1)} %reshape_reshape.3.bias_ref), custom_call_target="tpu_custom_call" | custom-call | flops 1811939328 | bytes 4718592 | tf_op jit(solution)/shard_map/pallas_call | solution.py:163
  101.1 0.7 copy-done.3
  101.8 0.7 copy-done.4
  102.5 0.6 copy-done.6
  103.2 117.9 %shard_map.121 = (bf16[384,1280]{1,0:T(8,128)(2,1)}, bf16[384,384]{1,0:T(8,128)(2,1)}, bf16[384,384]{1,0:T(8,128)(2,1)}, bf16[384,384]{1,0:T(8,128)(2,1)}, bf16[384,640]{1,0:T(8,128)(2,1)}) custom-call(bf16[384,384]{1,0:T(8,128)(2,1)} %q_ref.3, bf16[8,384,384]{2,1,0:T(8,128)(2,1)} %get-tuple-element.10.k_ref, bf16[8,384,384]{2,1,0:T(8,128)(2,1)} %get-tuple-element.11.v_ref, ...), custom_call_target="tpu_custom_call" | custom-call | tf_op jit(solution)/shard_map/pallas_call | solution.py:390
  221.1 2.3 copy.19
  223.4 1.7 copy.20
  225.1 1.7 copy.21
  226.8 1.7 copy.22
  228.5 0.8 copy.23
  (17 shorter events, 0.1 us)
Async XLA Ops:
  7.2 96.0 %all-gather.2.cloned.1.call-start = ((), (), s32[]{:S(2)}) async-start(), calls=%async_computation | async-start | bytes 4915200 | tf_op jit(solution)/shard_map/all_gather | solution.py:447
  12.8 90.4 %copy-start.5 = (f32[8,3,384]{2,1,0:T(4,128)}, f32[8,3,384]{2,1,0:T(4,128)S(1)}, u32[]{:S(2)}) copy-start(f32[8,3,384]{2,1,0:T(4,128)S(1)} %reshape_reshape.3.bias_ref) | copy-start | bytes 110596
  82.5 1.7 copy-start
  84.2 1.7 copy-start.1
  85.9 1.0 copy-start.2
  101.1 0.7 copy-start.3
  101.8 0.7 copy-start.4
  102.5 0.6 copy-start.6
  221.1 7.4 %copy-start.7 = (bf16[384,640]{1,0:T(8,128)(2,1)S(1)}, bf16[384,640]{1,0:T(8,128)(2,1)}, u32[]{:S(2)}) copy-start(bf16[384,640]{1,0:T(8,128)(2,1)} %get-tuple-element.24) | copy-start | bytes 1474564
Sparse Core Ops, SparseCore 0:
  9.6 34.5 all-gather.1

commit v3 on v2

--- a/solution.py
+++ b/solution.py
@@ -43,74 +43,102 @@
     z, x = me // nx, lax.rem(me, nx)
     line_barrier(nz, nx, z, x)
     items = ((k_ref, ko_ref), (v_ref, vo_ref))
-    started = []
-    for i, (src, dst) in enumerate(items):
+    sides = ((0, 1), (1, -1))
+
+    def x_copy(i, zz, px, dx, source):
+        shard = items[i][1].at[zz * nx + px]
+        return pltpu.make_async_remote_copy(
+            src_ref=shard if source is None else source, dst_ref=shard,
+            send_sem=xs.at[i, zz, dx - 1], recv_sem=xr.at[i, zz, dx - 1],
+            device_id={"seq": z * nx + lax.rem(x + dx, nx)}, device_id_type=MESH,
+        )
+
+    def z_copy(i, side, way, d, origin, source):
+        shard = items[i][1].at[origin * nx + x]
+        return pltpu.make_async_remote_copy(
+            src_ref=shard if source is None else source, dst_ref=shard,
+            send_sem=zs.at[i, side, d - 1], recv_sem=zr.at[i, side, d - 1],
+            device_id={"seq": lax.rem(z + way + nz, nz) * nx + x}, device_id_type=MESH,
+        )
+
+    def inside(p):
+        return (p >= 0) & (p < nz)
+
+    for i in range(2):
+        for side, way in sides:
+            @pl.when(inside(z + way))
+            def _():
+                z_copy(i, side, way, 1, z, items[i][0]).start()
         for dx in range(1, nx):
-            c = pltpu.make_async_remote_copy(
-                src_ref=src, dst_ref=dst.at[me],
-                send_sem=xs.at[i, 0, dx - 1], recv_sem=xr.at[i, 0, dx - 1],
-                device_id={"seq": z * nx + lax.rem(x + dx, nx)}, device_id_type=MESH,
-            )
-            c.start()
-            started.append(c)
-        for dz in range(1, nz):
-            c = pltpu.make_async_remote_copy(
-                src_ref=src, dst_ref=dst.at[me],
-                send_sem=zs.at[i, dz - 1], recv_sem=zr.at[i, dz - 1],
-                device_id={"seq": lax.rem(z + dz, nz) * nx + x}, device_id_type=MESH,
-            )
-            c.start()
-            started.append(c)
-    own = []
-    for i, (src, dst) in enumerate(items):
-        c = pltpu.make_async_copy(src, dst.at[me], own_sem.at[i])
-        c.start()
-        own.append(c)
-    for i, (src, dst) in enumerate(items):
-        for dz in range(1, nz):
-            s = lax.rem(z - dz + nz, nz) * nx + x
-            pltpu.make_async_remote_copy(
-                src_ref=src, dst_ref=dst.at[s],
-                send_sem=zs.at[i, dz - 1], recv_sem=zr.at[i, dz - 1],
-                device_id={"seq": s}, device_id_type=MESH,
-            ).wait_recv()
+            x_copy(i, z, x, dx, items[i][0]).start()
+        pltpu.make_async_copy(items[i][0], items[i][1].at[me], own_sem.at[i]).start()
+    for d in range(1, nz):
+        for i in range(2):
+            for side, way in sides:
+                origin = z - way * d
+
+                @pl.when(inside(origin))
+                def _():
+                    z_copy(i, side, way, d, origin, None).wait_recv()
+                    if d + 1 < nz:
+                        @pl.when(inside(z + way))
+                        def _():
+                            z_copy(i, side, way, d + 1, origin, None).start()
+                    for dx in range(1, nx):
+                        x_copy(i, origin, x, dx, None).start()
+    for i in range(2):
+        for zz in range(nz):
             for dx in range(1, nx):
-                c = pltpu.make_async_remote_copy(
-                    src_ref=dst.at[s], dst_ref=dst.at[s],
-                    send_sem=xs.at[i, dz, dx - 1], recv_sem=xr.at[i, dz, dx - 1],
-                    device_id={"seq": z * nx + lax.rem(x + dx, nx)}, device_id_type=MESH,
-                )
-                c.start()
-                started.append(c)
-    for i, (src, dst) in enumerate(items):
-        for dz in range(nz):
+                x_copy(i, zz, lax.rem(x - dx + nx, nx), dx, None).wait_recv()
+    for i in range(2):
+        for zz in range(nz):
             for dx in range(1, nx):
-                s = lax.rem(z - dz + nz, nz) * nx + lax.rem(x - dx + nx, nx)
-                pltpu.make_async_remote_copy(
-                    src_ref=src, dst_ref=dst.at[s],
-                    send_sem=xs.at[i, dz, dx - 1], recv_sem=xr.at[i, dz, dx - 1],
-                    device_id={"seq": z * nx + lax.rem(x + dx, nx)}, device_id_type=MESH,
-                ).wait_recv()
-    for c in started:
-        c.wait_send()
-    for c in own:
-        c.wait()
+                x_copy(i, zz, x, dx, None).wait_send()
+        for d in range(1, nz):
+            for side, way in sides:
+                origin = z - way * (d - 1)
+
+                @pl.when(inside(origin) & inside(z + way))
+                def _():
+                    z_copy(i, side, way, d, origin, None).wait_send()
+        pltpu.make_async_copy(items[i][0], items[i][1].at[me], own_sem.at[i]).wait()
 
 
 def gather_rows(keys, values, n_seq):
     nz, nx = NZ, n_seq // NZ
     shape = jax.ShapeDtypeStruct((n_seq,) + keys.shape, keys.dtype)
     dma = pltpu.SemaphoreType.DMA
+    z_sem, x_sem = dma((2, 2, nz - 1)), dma((2, nz, nx - 1))
     return pl.pallas_call(
         functools.partial(gather_kernel, nz, nx),
         out_shape=(shape, shape),
-        in_specs=[ANY, ANY],
-        out_specs=(ANY, ANY),
-        scratch_shapes=[
-            dma((2,)), dma((2, nz - 1)), dma((2, nz - 1)), dma((2, nz, nx - 1)), dma((2, nz, nx - 1)),
-        ],
-        compiler_params=pltpu.CompilerParams(collective_id=0, has_side_effects=True),
+        in_specs=[VMEM, VMEM],
+        out_specs=(VMEM, VMEM),
+        scratch_shapes=[dma((2,)), z_sem, z_sem, x_sem, x_sem],
+        compiler_params=pltpu.CompilerParams(
+            collective_id=0, has_side_effects=True, vmem_limit_bytes=24 * 2**20
+        ),
     )(keys, values)
+
+
+def store_kernel(n, *refs):
+    sems = refs[2 * n]
+    copies = [pltpu.make_async_copy(refs[i], refs[n + i], sems.at[i]) for i in range(n)]
+    for c in copies:
+        c.start()
+    for c in copies:
+        c.wait()
+
+
+def store(arrays):
+    n = len(arrays)
+    return pl.pallas_call(
+        functools.partial(store_kernel, n),
+        out_shape=tuple(jax.ShapeDtypeStruct(a.shape, a.dtype) for a in arrays),
+        in_specs=[VMEM] * n,
+        out_specs=(ANY,) * n,
+        scratch_shapes=[pltpu.SemaphoreType.DMA((n,))],
+    )(*arrays)
 
 
 def head(h):
@@ -175,7 +203,7 @@
             pl.BlockSpec((1, 8, rows), lambda h: (h, 0, 0)),
         ),
         scratch_shapes=[pltpu.VMEM((keys.shape[0], keys.shape[1], rows), f32)],
-        compiler_params=pltpu.CompilerParams(vmem_limit_bytes=48 * 2**20),
+        compiler_params=pltpu.CompilerParams(vmem_limit_bytes=24 * 2**20),
         cost_estimate=pl.CostEstimate(
             flops=flops, bytes_accessed=4 * keys.size, transcendentals=flops // (4 * HD)
         ),
@@ -447,8 +475,11 @@
     full_grad = lax.all_gather(d_output, "head", axis=1, tiled=True)
     all_keys, all_values = gather_rows(keys, values, n_seq)
     attn, attn_t, lse = forward(queries, all_keys, all_values, bias)
-    return backward(
-        n_seq, n_head, queries, all_keys, all_values, attn, attn_t, lse, bias, full_grad, out_weight
+    return store(
+        backward(
+            n_seq, n_head, queries, all_keys, all_values,
+            attn, attn_t, lse, bias, full_grad, out_weight,
+        )
     )
 
 

time: 237 us -> 216 us (0.911)
  Pallas kernels: 202 us -> 190 us
  local copies, waits for them, and re-layouts: 14.7 us -> 6.77 us
    pallas_call x1, Pallas kernels: 69.7 us -> 54.6 us  [gather_rows(): pl.pallas_call(functools.partial(gather_kernel, nz, nx), out_shape=(shape...]
    unnamed x21 -> x18, local copies, waits for them, and re-layouts: 14.5 us -> 6.56 us
    pallas_call x0 -> x1, Pallas kernels: none -> 3.03 us  [store(): pl.pallas_call(functools.partial(store_kernel, n), out_shape=tuple((jax.S...]
  transfers between devices with their start and end apart: 1 -> 1, of which waited for: 0 -> 0; matrix products, arithmetic and copies ran while one was open for 2% -> 2% of each run, Pallas kernels for 36% -> 32%
where the time goes in v3:
time: 216 us
  Pallas kernels  190 us (88%)
  between operations  14.8 us (7%)
  local copies, waits for them, and re-layouts  6.77 us (3%)
  other arithmetic  3.96 us (2%)
    pallas_call x1, Pallas kernels, backward(): pl.pallas_call(functools.partial(backward_kernel, nz, nx, nh), out_shape=...  118 us
    pallas_call x1, Pallas kernels, gather_rows(): pl.pallas_call(functools.partial(gather_kernel, nz, nx), out_shape=(shape...  54.6 us
    pallas_call x1, Pallas kernels, forward(): pl.pallas_call(forward_kernel, grid=(heads,), out_shape=(jax.ShapeDtypeSt...  14.3 us
    unnamed x18, local copies, waits for them, and re-layouts  6.56 us
  transfers between devices with their start and end apart: 1, of which 0 were waited for; matrix products, arithmetic and copies ran while one was open for 2% of the time, Pallas kernels for 32%

profile of v3, /device:TPU:9, one launch (start us, length us, event | category | flops | bytes accessed | tf_op | source)
XLA Modules:
  0.0 216.0 jit_solution(6131363357656430064)
XLA Ops:
  7.2 0.0 all-gather.2.cloned.1.call-start
  7.2 0.7 all-gather.2.cloned.1.call-update
  7.9 1.3 fusion.4
  9.9 0.8 select_reduce_fusion.2
  10.7 0.1 iota_compare_fusion.3
  10.8 0.8 select_reduce_fusion
  11.6 0.7 select_reduce_fusion.1
  12.3 0.1 iota_compare_fusion.2
  12.4 0.1 fusion.1
  12.5 0.1 copy.13
  12.6 0.1 broadcast_in_dim.77
  12.8 0.0 copy-start.5
  12.8 1.0 copy-done.5
  13.7 1.0 copy-done.6
  14.7 54.6 %shard_map.119 = (bf16[8,384,384]{2,1,0:T(8,128)(2,1)S(1)}, bf16[8,384,384]{2,1,0:T(8,128)(2,1)S(1)}) custom-call(bf16[384,384]{1,0:T(8,128)(2,1)S(1)} %copy-done.5, bf16[384,384]{1,0:T(8,128)(2,1)S(1)} %copy-done.6), custom_call_target="tpu_custom_call" | custom-call | tf_op jit(solution)/shard_map/pallas_call | solution.py:112
  69.3 0.0 copy-start.2
  69.3 1.2 copy-done.2
  70.5 14.3 %shard_map.120 = (bf16[384,384]{1,0:T(8,128)(2,1)S(1)}, bf16[384,384]{1,0:T(8,128)(2,1)S(1)}, f32[3,8,384]{2,1,0:T(8,128)S(1)}) custom-call(bf16[384,384]{1,0:T(8,128)(2,1)S(1)} %copy-done.2, bf16[8,384,384]{2,1,0:T(8,128)(2,1)S(1)} %get-tuple-element.15.k_ref, bf16[8,384,384]{2,1,0:T(8,128)(2,1)S(1)} %get-tuple-element.16.v_ref, ...), custom_call_target="tpu_custom_call" | custom-call | flops 1811939328 | bytes 4718592 | tf_op jit(solution)/shard_map/pallas_call | solution.py:191
  84.8 1.4 copy-done.1
  86.2 0.7 copy-done.3
  86.9 0.7 copy-done.4
  87.6 0.6 copy-done.8
  88.2 117.9 %shard_map.121 = (bf16[384,1280]{1,0:T(8,128)(2,1)}, bf16[384,384]{1,0:T(8,128)(2,1)}, bf16[384,384]{1,0:T(8,128)(2,1)}, bf16[384,384]{1,0:T(8,128)(2,1)}, bf16[384,640]{1,0:T(8,128)(2,1)}) custom-call(bf16[384,384]{1,0:T(8,128)(2,1)} %q_ref.3, bf16[8,384,384]{2,1,0:T(8,128)(2,1)} %copy-done, bf16[8,384,384]{2,1,0:T(8,128)(2,1)} %copy-done.1, ...), custom_call_target="tpu_custom_call" | custom-call | tf_op jit(solution)/shard_map/pallas_call | solution.py:418
  206.1 3.0 %shard_map.122 = (bf16[384,1280]{1,0:T(8,128)(2,1)}, bf16[384,384]{1,0:T(8,128)(2,1)}, bf16[384,384]{1,0:T(8,128)(2,1)}, bf16[384,384]{1,0:T(8,128)(2,1)}, bf16[384,640]{1,0:T(8,128)(2,1)}) custom-call(bf16[384,1280]{1,0:T(8,128)(2,1)} %get-tuple-element.20.refs_0_, bf16[384,384]{1,0:T(8,128)(2,1)} %get-tuple-element.21.refs_1_, ...), custom_call_target="tpu_custom_call" | custom-call | tf_op jit(solution)/shard_map/pallas_call | solution.py:135
  (15 shorter events, 0.1 us)
Async XLA Ops:
  7.2 81.1 %all-gather.2.cloned.1.call-start = ((), (), s32[]{:S(2)}) async-start(), calls=%async_computation | async-start | bytes 4915200 | tf_op jit(solution)/shard_map/all_gather | solution.py:475
  12.8 1.0 copy-start.5
  13.7 1.0 copy-start.6
  14.7 73.6 %copy-start.7 = (f32[8,3,384]{2,1,0:T(4,128)}, f32[8,3,384]{2,1,0:T(4,128)S(1)}, u32[]{:S(2)}) copy-start(f32[8,3,384]{2,1,0:T(4,128)S(1)} %reshape_reshape.3.bias_ref) | copy-start | bytes 110596
  69.3 19.0 %copy-start = (bf16[8,384,384]{2,1,0:T(8,128)(2,1)}, bf16[8,384,384]{2,1,0:T(8,128)(2,1)S(1)}, u32[]{:S(2)}) copy-start(bf16[8,384,384]{2,1,0:T(8,128)(2,1)S(1)} %get-tuple-element.15.k_ref) | copy-start | bytes 7077892
  69.3 1.2 copy-start.2
  84.8 1.4 copy-start.1
  86.2 0.7 copy-start.3
  86.9 0.7 copy-start.4
  87.6 0.6 copy-start.8
Sparse Core Ops, SparseCore 0:
  9.6 34.5 all-gather.1
